TPU v7x, 128 devices: a whole 4x4x4 slice. The times are simulated.
128 devices in a mesh: px: 8 (over z_hi, x), py: 16 (over z_lo, y, core).
Axes of the slice: x: 4, y: 4, z: 4 (z_hi: 2, z_lo: 2; z = z_hi * 2 + z_lo), core: 2. Of those that a mesh axis runs over, the one named last changes fastest.
Arguments:
- air_state: float32 [4, 32, 128, 1024], P(None, None, 'py', 'px'), may hold values from -6 to 6
- air_bulk: float32 [32, 128, 1024], P(None, 'py', 'px'), may hold values from 0.2 to 0.5
- air_buoyancy: float32 [32], replicated, may hold values from 0.3 to 0.6
- air_wind: float32 [2, 32], replicated, may hold values from 0.05 to 0.25
- ground_state: float32 [9, 16, 1024, 128], P(None, None, ('px', 'py')), may hold values from -6 to 6
- ground_moduli: float32 [2, 16, 1024, 128], P(None, None, ('px', 'py')), may hold values from 0.05 to 0.2
- ground_buoyancy: float32 [16, 1024, 128], P(None, ('px', 'py')), may hold values from 0.3 to 0.6
Outputs:
- air_after: float32 [4, 32, 128, 1024], P(None, None, 'py', 'px')
- ground_after: float32 [9, 16, 1024, 128], P(None, None, ('px', 'py'))
All inputs are finite; a program needn't handle non-finite values.
Results may differ from a plain program's by a relative error of at most 0.00002.
Values sent between devices are 32-bit elements; how exact they have to be, the bound alone decides.
A program may use at most 128 MiB of HBM per device.

v0:
```python
import jax
import jax.numpy as jnp
from jax import lax
from jax.sharding import PartitionSpec as P

STEPS = 3


def with_halo(block, sides, width):
    for axis, dim in sides:
        count = lax.axis_size(axis)
        forward = [(i, i + 1) for i in range(count - 1)]
        backward = [(target, source) for source, target in forward]
        low = lax.ppermute(
            lax.slice_in_dim(block, block.shape[dim] - width, None, axis=dim), axis, forward
        )
        high = lax.ppermute(lax.slice_in_dim(block, 0, width, axis=dim), axis, backward)
        block = jnp.concatenate([low, block, high], axis=dim)
    return block


def padded_2(array, sides, width):
    edges = {}
    for axis, dim in sides:
        size, length = (lax.axis_size(axis), array.shape[dim])
        up = [(i, (i + 1) % size) for i in range(size - 1)]
        last = lax.slice_in_dim(array, length - width, length, axis=dim)
        leading = lax.slice_in_dim(array, 0, width, axis=dim)
        edges[dim] = (
            lax.ppermute(last, axis, up),
            lax.ppermute(leading, axis, [(b, a) for a, b in up]),
        )
    done = []
    for _, dim in sides:
        low, high = edges[dim]
        around = [(width, width) if d in done else (0, 0) for d in range(array.ndim)]
        array = jnp.concatenate([jnp.pad(low, around), array, jnp.pad(high, around)], axis=dim)
        done.append(dim)
    return array


def middle(values):
    return values[:, 1:-1, 1:-1]


def beside(values, dimension, offset):
    if dimension == 1:
        return values[:, 1 + offset : values.shape[1] - 1 + offset, 1:-1]
    return values[:, 1:-1, 1 + offset : values.shape[2] - 1 + offset]


def lower_level(values):
    return jnp.concatenate([jnp.zeros_like(values[:1]), values[:-1]], 0)


def upper_level(values):
    return jnp.concatenate([values[1:], jnp.zeros_like(values[:1])], 0)


def clear_top(stress):
    component = lax.broadcasted_iota(jnp.int32, stress.shape, 0)
    layers = lax.broadcasted_iota(jnp.int32, stress.shape, 1)
    retain = (component < 4) | (layers < stress.shape[1] - 1)
    return jnp.where(retain, stress, jnp.zeros_like(stress))


def ground_velocity(velocity, padded_stress, buoyancy, pressure_plane, x_dim, y_dim):
    stress_xx = padded_stress[0]
    stress_yy = padded_stress[1]
    stress_zz = padded_stress[2]
    stress_xy = padded_stress[3]
    stress_xz = padded_stress[4]
    stress_yz = padded_stress[5]
    middle_xy = middle(stress_xy)
    middle_xz = middle(stress_xz)
    middle_yz = middle(stress_yz)
    middle_zz = middle(stress_zz)
    force_x = (
        beside(stress_xx, x_dim, 1)
        - middle(stress_xx)
        + middle_xy
        - beside(stress_xy, y_dim, -1)
        + middle_xz
        - lower_level(middle_xz)
    )
    force_y = (
        middle_xy
        - beside(stress_xy, x_dim, -1)
        + beside(stress_yy, y_dim, 1)
        - middle(stress_yy)
        + middle_yz
        - lower_level(middle_yz)
    )
    ghost_zz = jnp.concatenate([middle_zz[1:], -pressure_plane[None]], 0)
    force_z = (
        middle_xz
        - beside(stress_xz, x_dim, -1)
        + middle_yz
        - beside(stress_yz, y_dim, -1)
        + ghost_zz
        - middle_zz
    )
    return jnp.stack(
        [
            velocity[0] + buoyancy * force_x,
            velocity[1] + buoyancy * force_y,
            velocity[2] + buoyancy * force_z,
        ]
    )


def ground_stress(stress, padded_velocity, moduli, x_dim, y_dim):
    speed_x = padded_velocity[0]
    speed_y = padded_velocity[1]
    speed_z = padded_velocity[2]
    middle_x = middle(speed_x)
    middle_y = middle(speed_y)
    middle_z = middle(speed_z)
    lambda_mod = moduli[0]
    shear_mod = moduli[1]
    longitudinal = lambda_mod + 2.0 * shear_mod
    strain_x = middle_x - beside(speed_x, x_dim, -1)
    strain_y = middle_y - beside(speed_y, y_dim, -1)
    strain_z = middle_z - lower_level(middle_z)
    stress_xx = stress[0] + longitudinal * strain_x + lambda_mod * (strain_y + strain_z)
    stress_yy = stress[1] + longitudinal * strain_y + lambda_mod * (strain_x + strain_z)
    stress_zz = stress[2] + longitudinal * strain_z + lambda_mod * (strain_x + strain_y)
    stress_xy = stress[3] + shear_mod * (
        beside(speed_x, y_dim, 1) - middle_x + beside(speed_y, x_dim, 1) - middle_y
    )
    stress_xz = stress[4] + shear_mod * (
        upper_level(middle_x) - middle_x + beside(speed_z, x_dim, 1) - middle_z
    )
    stress_yz = stress[5] + shear_mod * (
        upper_level(middle_y) - middle_y + beside(speed_z, y_dim, 1) - middle_z
    )
    stress_xz = jnp.concatenate([stress_xz[:-1], jnp.zeros_like(stress_xz[-1:])], 0)
    stress_yz = jnp.concatenate([stress_yz[:-1], jnp.zeros_like(stress_yz[-1:])], 0)
    return jnp.stack([stress_xx, stress_yy, stress_zz, stress_xy, stress_xz, stress_yz])


def window(values, row_start, row_count, col_start, col_count):
    return values[:, row_start : row_start + row_count, col_start : col_start + col_count]


def air_update(air_field, bulk, buoyancy, wind, surface, west_inner, south_inner):
    row_count = air_field.shape[2]
    col_count = air_field.shape[3]
    padded = with_halo(air_field, (("px", 3), ("py", 2)), 2)
    pressure = padded[0]
    flow_x = padded[1]
    flow_y = padded[2]
    flow_z = padded[3]
    wind_x = wind[0][:, None, None]
    wind_y = wind[1][:, None, None]
    air_buoy = buoyancy[:, None, None]
    east = window(flow_x, 2, row_count, 1, col_count + 1)
    east_next = (
        east
        - wind_x * (east - window(flow_x, 2, row_count, 0, col_count + 1))
        - wind_y * (east - window(flow_x, 1, row_count, 1, col_count + 1))
        - air_buoy
        * (
            window(pressure, 2, row_count, 2, col_count + 1)
            - window(pressure, 2, row_count, 1, col_count + 1)
        )
    )
    east_next = jnp.concatenate(
        [
            jnp.where(west_inner, east_next[:, :, :1], jnp.zeros_like(east_next[:, :, :1])),
            east_next[:, :, 1:],
        ],
        2,
    )
    north = window(flow_y, 1, row_count + 1, 2, col_count)
    north_next = (
        north
        - wind_x * (north - window(flow_y, 1, row_count + 1, 1, col_count))
        - wind_y * (north - window(flow_y, 0, row_count + 1, 2, col_count))
        - air_buoy
        * (
            window(pressure, 2, row_count + 1, 2, col_count)
            - window(pressure, 1, row_count + 1, 2, col_count)
        )
    )
    north_next = jnp.concatenate(
        [
            jnp.where(south_inner, north_next[:, :1, :], jnp.zeros_like(north_next[:, :1, :])),
            north_next[:, 1:, :],
        ],
        1,
    )
    press_mid = window(pressure, 2, row_count, 2, col_count)
    upward = window(flow_z, 2, row_count, 2, col_count)
    upward_next = (
        upward
        - wind_x * (upward - window(flow_z, 2, row_count, 1, col_count))
        - wind_y * (upward - window(flow_z, 1, row_count, 2, col_count))
        - air_buoy * (press_mid - lower_level(press_mid))
    )
    upward_next = jnp.concatenate([surface[None], upward_next[1:]], 0)
    press_next = (
        press_mid
        - wind_x * (press_mid - window(pressure, 2, row_count, 1, col_count))
        - wind_y * (press_mid - window(pressure, 1, row_count, 2, col_count))
        - bulk
        * (
            east_next[:, :, 1:]
            - east_next[:, :, :-1]
            + (north_next[:, 1:, :] - north_next[:, :-1, :])
            + (upper_level(upward_next) - upward_next)
        )
    )
    return jnp.stack([press_next, east_next[:, :, 1:], north_next[:, 1:, :], upward_next])


def strip_rim(values):
    extended = padded_2(values, ((("px", "py"), 2),), 1)
    return jnp.pad(extended, ((0, 0), (0, 0), (0, 0), (1, 1)))


def body(air_state, air_bulk, air_buoyancy, air_wind, ground_state, ground_moduli, ground_buoyancy):
    west_inner = lax.axis_index("px") > 0
    south_inner = lax.axis_index("py") > 0
    air_field = air_state
    velocity = ground_state[:3]
    stress = clear_top(ground_state[3:])
    for iteration in range(STEPS):
        pressure_plane = lax.all_to_all(
            air_field[0, 0], "py", split_axis=1, concat_axis=0, tiled=True
        ).T
        velocity = ground_velocity(
            velocity, strip_rim(stress), ground_buoyancy, pressure_plane, 1, 2
        )
        surface = lax.all_to_all(velocity[2, -1], "py", split_axis=1, concat_axis=0, tiled=True).T
        air_field = air_update(
            air_field, air_bulk, air_buoyancy, air_wind, surface, west_inner, south_inner
        )
        stress = ground_stress(stress, strip_rim(velocity), ground_moduli, 1, 2)
    ground = jnp.concatenate([velocity, stress], 0)
    return (air_field, ground)


def solution(mesh):
    placed = (
        P(None, None, "py", "px"),
        P(None, "py", "px"),
        P(),
        P(),
        P(None, None, ("px", "py"), None),
        P(None, None, ("px", "py"), None),
        P(None, ("px", "py"), None),
    )
    return jax.shard_map(
        body,
        mesh=mesh,
        in_specs=placed,
        out_specs=(P(None, None, "py", "px"), P(None, None, ("px", "py"), None)),
        check_vma=False,
    )
```

profile of v0, /device:TPU:96, one launch (start us, length us, event | category | flops | bytes accessed | tf_op | source)
XLA Modules:
  0.0 198.7 jit_solution(9225862727669534803)
XLA Ops:
  2.1 5.9 %all-to-all-start = ((f32[8,16,8]{2,0,1:T(8,128)}), f32[8,16,8]{2,0,1:T(8,128)S(1)}, u32[]{:S(2)}, u32[]{:S(2)}) async-start(f32[8,16,8]{2,0,1:T(8,128)} %copy.21), calls=%async_computation | async-start | bytes 131072 | tf_op jit(solution)/shard_map/all_to_all | solution.py:229
  11.2 5.6 %collective-permute-start.5 = (f32[6,16,1,128]{3,2,1,0:T(1,128)S(1)}, f32[6,16,1,128]{3,2,1,0:T(1,128)S(1)}, u32[]{:S(2)}, u32[]{:S(2)}) collective-permute-start(f32[6,16,1,128]{3,2,1,0:T(1,128)S(1)} %get-tuple-element.99), channel_id=1, source_target_pairs={{1,0},{2,1},{3,2},{4,3},{5,4},{6,5},{7,6},{8,7},{9,8},{10,9},{11,1... | collective-permute-start | bytes 147464 | tf_op jit(solution)/shard_map/ppermute | solution.py:31
  16.9 2.3 %fusion.206 = (f32[4,32,8,2]{3,2,1,0:T(8,128)}, f32[4,32,8,2]{3,2,1,0:T(8,128)S(1)}) fusion(f32[4,32,8,128]{3,2,1,0:T(8,128)} %param.7), kind=kLoop, calls=%fused_computation.423 | loop fusion | bytes 32768 | tf_op jit(solution)/shard_map/slice | solution.py:15
  19.2 3.4 %collective-permute-start = (f32[4,32,8,2]{3,2,1,0:T(8,128)}, f32[4,32,8,2]{3,2,1,0:T(8,128)S(1)}, u32[]{:S(2)}, u32[]{:S(2)}) collective-permute-start(f32[4,32,8,2]{3,2,1,0:T(8,128)} %get-tuple-element.92), channel_id=1, source_target_pairs={{0,16},{16,32},{32,48},{48,64},{64,80},{80,96},{96,112},{1,17},{17... | collective-permute-start | bytes 24584 | tf_op jit(solution)/shard_map/ppermute | solution.py:14
  22.6 6.1 %collective-permute-start.1 = (f32[4,32,8,2]{3,2,1,0:T(8,128)S(1)}, f32[4,32,8,2]{3,2,1,0:T(8,128)S(1)}, u32[]{:S(2)}, u32[]{:S(2)}) collective-permute-start(f32[4,32,8,2]{3,2,1,0:T(8,128)S(1)} %get-tuple-element.93), channel_id=1, source_target_pairs={{16,0},{32,16},{48,32},{64,48},{80,64},{96,80},{112,96},{17,1},{33... | collective-permute-start | bytes 24584 | tf_op jit(solution)/shard_map/ppermute | solution.py:17
  34.6 5.8 %collective-permute-start.11 = (f32[3,16,1,128]{3,2,1,0:T(1,128)S(1)}, f32[3,16,1,128]{3,2,1,0:T(1,128)S(1)}, u32[]{:S(2)}, u32[]{:S(2)}) collective-permute-start(f32[3,16,1,128]{3,2,1,0:T(1,128)S(1)} %get-tuple-element.119), channel_id=1, source_target_pairs={{1,0},{2,1},{3,2},{4,3},{5,4},{6,5},{7,6},{8,7},{9,8},{10,9},{11,1... | collective-permute-start | bytes 73736 | tf_op jit(solution)/shard_map/ppermute | solution.py:31
  43.0 7.6 %all-to-all-start.1 = ((f32[8,16,8]{2,0,1:T(8,128)}), f32[8,16,8]{2,0,1:T(8,128)S(1)}, u32[]{:S(2)}, u32[]{:S(2)}) async-start(f32[8,16,8]{2,0,1:T(8,128)} %copy.23), calls=%async_computation.1 | async-start | bytes 131072 | tf_op jit(solution)/shard_map/all_to_all | solution.py:235
  54.9 2.0 %collective-permute-start.12 = (f32[6,16,1,128]{3,2,1,0:T(1,128)S(1)}, f32[6,16,1,128]{3,2,1,0:T(1,128)S(1)}, u32[]{:S(2)}, u32[]{:S(2)}) collective-permute-start(f32[6,16,1,128]{3,2,1,0:T(1,128)S(1)} %get-tuple-element.96), channel_id=1, source_target_pairs={{0,1},{1,2},{2,3},{3,4},{4,5},{5,6},{6,7},{7,8},{8,9},{9,10},{10,1... | collective-permute-start | bytes 147464 | tf_op jit(solution)/shard_map/ppermute | solution.py:30
  56.9 5.6 %collective-permute-start.13 = (f32[6,16,1,128]{3,2,1,0:T(1,128)S(1)}, f32[6,16,1,128]{3,2,1,0:T(1,128)S(1)}, u32[]{:S(2)}, u32[]{:S(2)}) collective-permute-start(f32[6,16,1,128]{3,2,1,0:T(1,128)S(1)} %get-tuple-element.97), channel_id=1, source_target_pairs={{1,0},{2,1},{3,2},{4,3},{5,4},{6,5},{7,6},{8,7},{9,8},{10,9},{11,1... | collective-permute-start | bytes 147464 | tf_op jit(solution)/shard_map/ppermute | solution.py:31
  66.2 5.8 %collective-permute-start.3 = (f32[4,32,2,132]{3,2,1,0:T(2,128)}, f32[4,32,2,132]{3,2,1,0:T(2,128)}, u32[]{:S(2)}, u32[]{:S(2)}) collective-permute-start(f32[4,32,2,132]{3,2,1,0:T(2,128)} %get-tuple-element.67), channel_id=1, source_target_pairs={{1,0},{2,1},{3,2},{4,3},{5,4},{6,5},{7,6},{8,7},{9,8},{10,9},{11,1... | collective-permute-start | bytes 405512 | tf_op jit(solution)/shard_map/ppermute | solution.py:17
  76.2 2.0 %pad_maximum_fusion = f32[4,32,12,132]{3,2,1,0:T(8,128)S(1)} fusion(f32[4,32,2,132]{3,2,1,0:T(2,128)} %collective-permute-done.3, f32[4,32,8,2]{3,2,1,0:T(8,128)S(1)} %collective-permute-done.1, f32[4,32,8,128]{3,2,1,0:T(8,128)S(1)} %copy-done.1, f32[4,32,8,2]{3,2,1,0:T(8,128)S(1)} %collective-permute-done, f32[4,32,2,132]{3,2,1,0:T(2,128)} %collective-permute-done.2), kind=kLoop, calls=%fused_computation.2 | loop fusion | flops 811008 | bytes 1622016 | tf_op jit(solution)/shard_map/concatenate | solution.py:18
  81.2 5.9 %all-to-all-start.2 = ((f32[8,16,8]{2,0,1:T(8,128)}), f32[8,16,8]{2,0,1:T(8,128)S(1)}, u32[]{:S(2)}, u32[]{:S(2)}) async-start(f32[8,16,8]{2,0,1:T(8,128)} %copy.25), calls=%async_computation.2 | async-start | bytes 131072 | tf_op jit(solution)/shard_map/all_to_all | solution.py:229
  87.1 4.8 %all-to-all-done.2 = f32[8,16,8]{2,0,1:T(8,128)S(1)} async-done(((f32[8,16,8]{2,0,1:T(8,128)}), f32[8,16,8]{2,0,1:T(8,128)S(1)}, u32[]{:S(2)}, u32[]{:S(2)}) %all-to-all-start.2) | async-done | bytes 4128 | tf_op jit(solution)/shard_map/all_to_all | solution.py:229
  92.9 4.7 %all-to-all-start.3 = ((f32[8,16,8]{2,0,1:T(8,128)}), f32[8,16,8]{2,0,1:T(8,128)S(1)}, u32[]{:S(2)}, u32[]{:S(2)}) async-start(f32[8,16,8]{2,0,1:T(8,128)} %copy.27), calls=%async_computation.3 | async-start | bytes 131072 | tf_op jit(solution)/shard_map/all_to_all | solution.py:235
  99.7 5.6 %collective-permute-start.19 = (f32[3,16,1,128]{3,2,1,0:T(1,128)S(1)}, f32[3,16,1,128]{3,2,1,0:T(1,128)S(1)}, u32[]{:S(2)}, u32[]{:S(2)}) collective-permute-start(f32[3,16,1,128]{3,2,1,0:T(1,128)S(1)} %get-tuple-element.117), channel_id=1, source_target_pairs={{1,0},{2,1},{3,2},{4,3},{5,4},{6,5},{7,6},{8,7},{9,8},{10,9},{11,1... | collective-permute-start | bytes 73736 | tf_op jit(solution)/shard_map/ppermute | solution.py:31
  108.3 7.7 %collective-permute-start.7 = (f32[4,32,8,2]{3,2,1,0:T(8,128)S(1)}, f32[4,32,8,2]{3,2,1,0:T(8,128)S(1)}, u32[]{:S(2)}, u32[]{:S(2)}) collective-permute-start(f32[4,32,8,2]{3,2,1,0:T(8,128)S(1)} %get-tuple-element.88), channel_id=1, source_target_pairs={{16,0},{32,16},{48,32},{64,48},{80,64},{96,80},{112,96},{17,1},{33... | collective-permute-start | bytes 24584 | tf_op jit(solution)/shard_map/ppermute | solution.py:17
  125.1 5.8 %collective-permute-start.21 = (f32[6,16,1,128]{3,2,1,0:T(1,128)S(1)}, f32[6,16,1,128]{3,2,1,0:T(1,128)S(1)}, u32[]{:S(2)}, u32[]{:S(2)}) collective-permute-start(f32[6,16,1,128]{3,2,1,0:T(1,128)S(1)} %get-tuple-element.95), channel_id=1, source_target_pairs={{1,0},{2,1},{3,2},{4,3},{5,4},{6,5},{7,6},{8,7},{9,8},{10,9},{11,1... | collective-permute-start | bytes 147464 | tf_op jit(solution)/shard_map/ppermute | solution.py:31
  133.7 5.8 %collective-permute-start.9 = (f32[4,32,2,132]{3,2,1,0:T(2,128)S(1)}, f32[4,32,2,132]{3,2,1,0:T(2,128)S(1)}, u32[]{:S(2)}, u32[]{:S(2)}) collective-permute-start(f32[4,32,2,132]{3,2,1,0:T(2,128)S(1)} %get-tuple-element.65), channel_id=1, source_target_pairs={{1,0},{2,1},{3,2},{4,3},{5,4},{6,5},{7,6},{8,7},{9,8},{10,9},{11,1... | collective-permute-start | bytes 405512 | tf_op jit(solution)/shard_map/ppermute | solution.py:17
  147.4 5.9 %all-to-all-start.4 = ((f32[8,16,8]{2,0,1:T(8,128)}), f32[8,16,8]{2,0,1:T(8,128)S(1)}, u32[]{:S(2)}, u32[]{:S(2)}) async-start(f32[8,16,8]{2,0,1:T(8,128)} %copy.29), calls=%async_computation.4 | async-start | bytes 131072 | tf_op jit(solution)/shard_map/all_to_all | solution.py:229
  156.3 7.5 %collective-permute-start.15 = (f32[4,32,8,2]{3,2,1,0:T(8,128)}, f32[4,32,8,2]{3,2,1,0:T(8,128)S(1)}, u32[]{:S(2)}, u32[]{:S(2)}) collective-permute-start(f32[4,32,8,2]{3,2,1,0:T(8,128)} %get-tuple-element.83), channel_id=1, source_target_pairs={{16,0},{32,16},{48,32},{64,48},{80,64},{96,80},{112,96},{17,1},{33... | collective-permute-start | bytes 24584 | tf_op jit(solution)/shard_map/ppermute | solution.py:17
  166.4 5.7 %all-to-all-start.5 = ((f32[8,16,8]{2,0,1:T(8,128)}), f32[8,16,8]{2,0,1:T(8,128)S(1)}, u32[]{:S(2)}, u32[]{:S(2)}) async-start(f32[8,16,8]{2,0,1:T(8,128)} %copy.31), calls=%async_computation.5 | async-start | bytes 131072 | tf_op jit(solution)/shard_map/all_to_all | solution.py:235
  174.2 5.6 %collective-permute-start.23 = (f32[3,16,1,128]{3,2,1,0:T(1,128)S(1)}, f32[3,16,1,128]{3,2,1,0:T(1,128)S(1)}, u32[]{:S(2)}, u32[]{:S(2)}) collective-permute-start(f32[3,16,1,128]{3,2,1,0:T(1,128)S(1)} %get-tuple-element.115), channel_id=1, source_target_pairs={{1,0},{2,1},{3,2},{4,3},{5,4},{6,5},{7,6},{8,7},{9,8},{10,9},{11,1... | collective-permute-start | bytes 73736 | tf_op jit(solution)/shard_map/ppermute | solution.py:31
  180.9 2.1 %collective-permute-start.16 = (f32[4,32,2,132]{3,2,1,0:T(2,128)S(1)}, f32[4,32,2,132]{3,2,1,0:T(2,128)S(1)}, u32[]{:S(2)}, u32[]{:S(2)}) collective-permute-start(f32[4,32,2,132]{3,2,1,0:T(2,128)S(1)} %get-tuple-element.56), channel_id=1, source_target_pairs={{0,1},{1,2},{2,3},{3,4},{4,5},{5,6},{6,7},{7,8},{8,9},{9,10},{10,1... | collective-permute-start | bytes 405512 | tf_op jit(solution)/shard_map/ppermute | solution.py:14
  182.9 6.1 %collective-permute-start.17 = (f32[4,32,2,132]{3,2,1,0:T(2,128)S(1)}, f32[4,32,2,132]{3,2,1,0:T(2,128)S(1)}, u32[]{:S(2)}, u32[]{:S(2)}) collective-permute-start(f32[4,32,2,132]{3,2,1,0:T(2,128)S(1)} %get-tuple-element.57), channel_id=1, source_target_pairs={{1,0},{2,1},{3,2},{4,3},{5,4},{6,5},{7,6},{8,7},{9,8},{10,9},{11,1... | collective-permute-start | bytes 405512 | tf_op jit(solution)/shard_map/ppermute | solution.py:17
  (234 shorter events, 71.4 us)
Async XLA Ops:
  2.1 26.6 %all-to-all-start = ((f32[8,16,8]{2,0,1:T(8,128)}), f32[8,16,8]{2,0,1:T(8,128)S(1)}, u32[]{:S(2)}, u32[]{:S(2)}) async-start(f32[8,16,8]{2,0,1:T(8,128)} %copy.21), calls=%async_computation | async-start | bytes 131072 | tf_op jit(solution)/shard_map/all_to_all | solution.py:229
  9.2 19.5 %collective-permute-start.4 = (f32[6,16,1,128]{3,2,1,0:T(1,128)S(1)}, f32[6,16,1,128]{3,2,1,0:T(1,128)S(1)}, u32[]{:S(2)}, u32[]{:S(2)}) collective-permute-start(f32[6,16,1,128]{3,2,1,0:T(1,128)S(1)} %get-tuple-element.98), channel_id=1, source_target_pairs={{0,1},{1,2},{2,3},{3,4},{4,5},{5,6},{6,7},{7,8},{8,9},{9,10},{10,1... | collective-permute-start | bytes 147464 | tf_op jit(solution)/shard_map/ppermute | solution.py:30
  11.2 17.5 %collective-permute-start.5 = (f32[6,16,1,128]{3,2,1,0:T(1,128)S(1)}, f32[6,16,1,128]{3,2,1,0:T(1,128)S(1)}, u32[]{:S(2)}, u32[]{:S(2)}) collective-permute-start(f32[6,16,1,128]{3,2,1,0:T(1,128)S(1)} %get-tuple-element.99), channel_id=1, source_target_pairs={{1,0},{2,1},{3,2},{4,3},{5,4},{6,5},{7,6},{8,7},{9,8},{10,9},{11,1... | collective-permute-start | bytes 147464 | tf_op jit(solution)/shard_map/ppermute | solution.py:31
  19.2 43.4 %collective-permute-start = (f32[4,32,8,2]{3,2,1,0:T(8,128)}, f32[4,32,8,2]{3,2,1,0:T(8,128)S(1)}, u32[]{:S(2)}, u32[]{:S(2)}) collective-permute-start(f32[4,32,8,2]{3,2,1,0:T(8,128)} %get-tuple-element.92), channel_id=1, source_target_pairs={{0,16},{16,32},{32,48},{48,64},{64,80},{80,96},{96,112},{1,17},{17... | collective-permute-start | bytes 24584 | tf_op jit(solution)/shard_map/ppermute | solution.py:14
  22.6 40.0 %collective-permute-start.1 = (f32[4,32,8,2]{3,2,1,0:T(8,128)S(1)}, f32[4,32,8,2]{3,2,1,0:T(8,128)S(1)}, u32[]{:S(2)}, u32[]{:S(2)}) collective-permute-start(f32[4,32,8,2]{3,2,1,0:T(8,128)S(1)} %get-tuple-element.93), channel_id=1, source_target_pairs={{16,0},{32,16},{48,32},{64,48},{80,64},{96,80},{112,96},{17,1},{33... | collective-permute-start | bytes 24584 | tf_op jit(solution)/shard_map/ppermute | solution.py:17
  32.7 18.0 %collective-permute-start.10 = (f32[3,16,1,128]{3,2,1,0:T(1,128)S(1)}, f32[3,16,1,128]{3,2,1,0:T(1,128)S(1)}, u32[]{:S(2)}, u32[]{:S(2)}) collective-permute-start(f32[3,16,1,128]{3,2,1,0:T(1,128)S(1)} %get-tuple-element.118), channel_id=1, source_target_pairs={{0,1},{1,2},{2,3},{3,4},{4,5},{5,6},{6,7},{7,8},{8,9},{9,10},{10,1... | collective-permute-start | bytes 73736 | tf_op jit(solution)/shard_map/ppermute | solution.py:30
  34.6 16.1 %collective-permute-start.11 = (f32[3,16,1,128]{3,2,1,0:T(1,128)S(1)}, f32[3,16,1,128]{3,2,1,0:T(1,128)S(1)}, u32[]{:S(2)}, u32[]{:S(2)}) collective-permute-start(f32[3,16,1,128]{3,2,1,0:T(1,128)S(1)} %get-tuple-element.119), channel_id=1, source_target_pairs={{1,0},{2,1},{3,2},{4,3},{5,4},{6,5},{7,6},{8,7},{9,8},{10,9},{11,1... | collective-permute-start | bytes 73736 | tf_op jit(solution)/shard_map/ppermute | solution.py:31
  43.0 29.0 %all-to-all-start.1 = ((f32[8,16,8]{2,0,1:T(8,128)}), f32[8,16,8]{2,0,1:T(8,128)S(1)}, u32[]{:S(2)}, u32[]{:S(2)}) async-start(f32[8,16,8]{2,0,1:T(8,128)} %copy.23), calls=%async_computation.1 | async-start | bytes 131072 | tf_op jit(solution)/shard_map/all_to_all | solution.py:235
  54.9 17.7 %collective-permute-start.12 = (f32[6,16,1,128]{3,2,1,0:T(1,128)S(1)}, f32[6,16,1,128]{3,2,1,0:T(1,128)S(1)}, u32[]{:S(2)}, u32[]{:S(2)}) collective-permute-start(f32[6,16,1,128]{3,2,1,0:T(1,128)S(1)} %get-tuple-element.96), channel_id=1, source_target_pairs={{0,1},{1,2},{2,3},{3,4},{4,5},{5,6},{6,7},{7,8},{8,9},{9,10},{10,1... | collective-permute-start | bytes 147464 | tf_op jit(solution)/shard_map/ppermute | solution.py:30
  56.9 15.7 %collective-permute-start.13 = (f32[6,16,1,128]{3,2,1,0:T(1,128)S(1)}, f32[6,16,1,128]{3,2,1,0:T(1,128)S(1)}, u32[]{:S(2)}, u32[]{:S(2)}) collective-permute-start(f32[6,16,1,128]{3,2,1,0:T(1,128)S(1)} %get-tuple-element.97), channel_id=1, source_target_pairs={{1,0},{2,1},{3,2},{4,3},{5,4},{6,5},{7,6},{8,7},{9,8},{10,9},{11,1... | collective-permute-start | bytes 147464 | tf_op jit(solution)/shard_map/ppermute | solution.py:31
  92.9 23.1 %all-to-all-start.3 = ((f32[8,16,8]{2,0,1:T(8,128)}), f32[8,16,8]{2,0,1:T(8,128)S(1)}, u32[]{:S(2)}, u32[]{:S(2)}) async-start(f32[8,16,8]{2,0,1:T(8,128)} %copy.27), calls=%async_computation.3 | async-start | bytes 131072 | tf_op jit(solution)/shard_map/all_to_all | solution.py:235
  97.7 19.0 %collective-permute-start.18 = (f32[3,16,1,128]{3,2,1,0:T(1,128)S(1)}, f32[3,16,1,128]{3,2,1,0:T(1,128)S(1)}, u32[]{:S(2)}, u32[]{:S(2)}) collective-permute-start(f32[3,16,1,128]{3,2,1,0:T(1,128)S(1)} %get-tuple-element.116), channel_id=1, source_target_pairs={{0,1},{1,2},{2,3},{3,4},{4,5},{5,6},{6,7},{7,8},{8,9},{9,10},{10,1... | collective-permute-start | bytes 73736 | tf_op jit(solution)/shard_map/ppermute | solution.py:30
  99.7 17.0 %collective-permute-start.19 = (f32[3,16,1,128]{3,2,1,0:T(1,128)S(1)}, f32[3,16,1,128]{3,2,1,0:T(1,128)S(1)}, u32[]{:S(2)}, u32[]{:S(2)}) collective-permute-start(f32[3,16,1,128]{3,2,1,0:T(1,128)S(1)} %get-tuple-element.117), channel_id=1, source_target_pairs={{1,0},{2,1},{3,2},{4,3},{5,4},{6,5},{7,6},{8,7},{9,8},{10,9},{11,1... | collective-permute-start | bytes 73736 | tf_op jit(solution)/shard_map/ppermute | solution.py:31
  106.4 24.5 %collective-permute-start.6 = (f32[4,32,8,2]{3,2,1,0:T(8,128)}, f32[4,32,8,2]{3,2,1,0:T(8,128)S(1)}, u32[]{:S(2)}, u32[]{:S(2)}) collective-permute-start(f32[4,32,8,2]{3,2,1,0:T(8,128)} %get-tuple-element.87), channel_id=1, source_target_pairs={{0,16},{16,32},{32,48},{48,64},{64,80},{80,96},{96,112},{1,17},{17... | collective-permute-start | bytes 24584 | tf_op jit(solution)/shard_map/ppermute | solution.py:14
  108.3 22.6 %collective-permute-start.7 = (f32[4,32,8,2]{3,2,1,0:T(8,128)S(1)}, f32[4,32,8,2]{3,2,1,0:T(8,128)S(1)}, u32[]{:S(2)}, u32[]{:S(2)}) collective-permute-start(f32[4,32,8,2]{3,2,1,0:T(8,128)S(1)} %get-tuple-element.88), channel_id=1, source_target_pairs={{16,0},{32,16},{48,32},{64,48},{80,64},{96,80},{112,96},{17,1},{33... | collective-permute-start | bytes 24584 | tf_op jit(solution)/shard_map/ppermute | solution.py:17
  123.2 16.3 %collective-permute-start.20 = (f32[6,16,1,128]{3,2,1,0:T(1,128)S(1)}, f32[6,16,1,128]{3,2,1,0:T(1,128)S(1)}, u32[]{:S(2)}, u32[]{:S(2)}) collective-permute-start(f32[6,16,1,128]{3,2,1,0:T(1,128)S(1)} %get-tuple-element.94), channel_id=1, source_target_pairs={{0,1},{1,2},{2,3},{3,4},{4,5},{5,6},{6,7},{7,8},{8,9},{9,10},{10,1... | collective-permute-start | bytes 147464 | tf_op jit(solution)/shard_map/ppermute | solution.py:30
  125.1 14.4 %collective-permute-start.21 = (f32[6,16,1,128]{3,2,1,0:T(1,128)S(1)}, f32[6,16,1,128]{3,2,1,0:T(1,128)S(1)}, u32[]{:S(2)}, u32[]{:S(2)}) collective-permute-start(f32[6,16,1,128]{3,2,1,0:T(1,128)S(1)} %get-tuple-element.95), channel_id=1, source_target_pairs={{1,0},{2,1},{3,2},{4,3},{5,4},{6,5},{7,6},{8,7},{9,8},{10,9},{11,1... | collective-permute-start | bytes 147464 | tf_op jit(solution)/shard_map/ppermute | solution.py:31
  147.4 16.5 %all-to-all-start.4 = ((f32[8,16,8]{2,0,1:T(8,128)}), f32[8,16,8]{2,0,1:T(8,128)S(1)}, u32[]{:S(2)}, u32[]{:S(2)}) async-start(f32[8,16,8]{2,0,1:T(8,128)} %copy.29), calls=%async_computation.4 | async-start | bytes 131072 | tf_op jit(solution)/shard_map/all_to_all | solution.py:229
  154.4 25.5 %collective-permute-start.14 = (f32[4,32,8,2]{3,2,1,0:T(8,128)}, f32[4,32,8,2]{3,2,1,0:T(8,128)S(1)}, u32[]{:S(2)}, u32[]{:S(2)}) collective-permute-start(f32[4,32,8,2]{3,2,1,0:T(8,128)} %get-tuple-element.82), channel_id=1, source_target_pairs={{0,16},{16,32},{32,48},{48,64},{64,80},{80,96},{96,112},{1,17},{17... | collective-permute-start | bytes 24584 | tf_op jit(solution)/shard_map/ppermute | solution.py:14
  156.3 23.6 %collective-permute-start.15 = (f32[4,32,8,2]{3,2,1,0:T(8,128)}, f32[4,32,8,2]{3,2,1,0:T(8,128)S(1)}, u32[]{:S(2)}, u32[]{:S(2)}) collective-permute-start(f32[4,32,8,2]{3,2,1,0:T(8,128)} %get-tuple-element.83), channel_id=1, source_target_pairs={{16,0},{32,16},{48,32},{64,48},{80,64},{96,80},{112,96},{17,1},{33... | collective-permute-start | bytes 24584 | tf_op jit(solution)/shard_map/ppermute | solution.py:17
  166.4 13.4 %all-to-all-start.5 = ((f32[8,16,8]{2,0,1:T(8,128)}), f32[8,16,8]{2,0,1:T(8,128)S(1)}, u32[]{:S(2)}, u32[]{:S(2)}) async-start(f32[8,16,8]{2,0,1:T(8,128)} %copy.31), calls=%async_computation.5 | async-start | bytes 131072 | tf_op jit(solution)/shard_map/all_to_all | solution.py:235
  172.2 16.9 %collective-permute-start.22 = (f32[3,16,1,128]{3,2,1,0:T(1,128)S(1)}, f32[3,16,1,128]{3,2,1,0:T(1,128)S(1)}, u32[]{:S(2)}, u32[]{:S(2)}) collective-permute-start(f32[3,16,1,128]{3,2,1,0:T(1,128)S(1)} %get-tuple-element.114), channel_id=1, source_target_pairs={{0,1},{1,2},{2,3},{3,4},{4,5},{5,6},{6,7},{7,8},{8,9},{9,10},{10,1... | collective-permute-start | bytes 73736 | tf_op jit(solution)/shard_map/ppermute | solution.py:30
  174.2 14.8 %collective-permute-start.23 = (f32[3,16,1,128]{3,2,1,0:T(1,128)S(1)}, f32[3,16,1,128]{3,2,1,0:T(1,128)S(1)}, u32[]{:S(2)}, u32[]{:S(2)}) collective-permute-start(f32[3,16,1,128]{3,2,1,0:T(1,128)S(1)} %get-tuple-element.115), channel_id=1, source_target_pairs={{1,0},{2,1},{3,2},{4,3},{5,4},{6,5},{7,6},{8,7},{9,8},{10,9},{11,1... | collective-permute-start | bytes 73736 | tf_op jit(solution)/shard_map/ppermute | solution.py:31
  180.9 13.7 %collective-permute-start.16 = (f32[4,32,2,132]{3,2,1,0:T(2,128)S(1)}, f32[4,32,2,132]{3,2,1,0:T(2,128)S(1)}, u32[]{:S(2)}, u32[]{:S(2)}) collective-permute-start(f32[4,32,2,132]{3,2,1,0:T(2,128)S(1)} %get-tuple-element.56), channel_id=1, source_target_pairs={{0,1},{1,2},{2,3},{3,4},{4,5},{5,6},{6,7},{7,8},{8,9},{9,10},{10,1... | collective-permute-start | bytes 405512 | tf_op jit(solution)/shard_map/ppermute | solution.py:14
  (34 other events, 207.7 us)
where the time goes:
time: 200 us; the launch traced here: 199 us
  starting transfers between devices  134 us (67%)
  other arithmetic  37.5 us (19%)
  local copies, waits for them, and re-layouts  19 us (10%)
  waiting for transfers between devices  6.45 us (3%)
    ppermute x6, starting transfers between devices, with_halo(): lax.ppermute(lax.slice_in_dim(block, 0, width, axis=dim), axis, backward)  38.9 us
    ppermute x6, starting transfers between devices, padded_2(): lax.ppermute(leading, axis, [(b, a) for a, b in up])  34.1 us
    all_to_all x3, starting transfers between devices, body(): lax.all_to_all(velocity[2, -1], 'py', split_axis=1, concat_axis=0, tiled=...  18.1 us
    all_to_all x3, starting transfers between devices, body(): lax.all_to_all(air_field[0, 0], 'py', split_axis=1, concat_axis=0, tiled=...  17.7 us
    unnamed x18, other arithmetic  15.8 us
    ppermute x6, starting transfers between devices, with_halo(): lax.ppermute(lax.slice_in_dim(block, block.shape[dim] - width, None, axis...  13.1 us
    ppermute x6, starting transfers between devices, padded_2(): lax.ppermute(last, axis, up)  12 us
    all_to_all x3, waiting for transfers between devices, body(): lax.all_to_all(air_field[0, 0], 'py', split_axis=1, concat_axis=0, tiled=...  4.81 us
  transfers between devices with their start and end apart: 30, of which 3 were waited for; matrix products, arithmetic and copies ran while one was open for 21% of the time, Pallas kernels for 0%

commit v1 on v0

--- a/solution.py
+++ b/solution.py
@@ -232,7 +232,13 @@
         velocity = ground_velocity(
             velocity, strip_rim(stress), ground_buoyancy, pressure_plane, 1, 2
         )
-        surface = lax.all_to_all(velocity[2, -1], "py", split_axis=1, concat_axis=0, tiled=True).T
+        assign_body = lambda row_data: jnp.concatenate(
+            lax.all_to_all(
+                jnp.stack(jnp.split(row_data, lax.axis_size("py"), axis=1), axis=0), "py", 0, 0
+            ),
+            axis=0,
+        )
+        surface = assign_body(velocity[2, -1]).T
         air_field = air_update(
             air_field, air_bulk, air_buoyancy, air_wind, surface, west_inner, south_inner
         )

time: 200 us -> 232 us (1.16)
  local copies, waits for them, and re-layouts: 19 us -> 48.3 us
    unnamed x56 -> x101, local copies, waits for them, and re-layouts: 0.46 us -> 30 us
    all_to_all x9 -> x0, local copies, waits for them, and re-layouts: 3.55 us -> none  [body(): lax.all_to_all(velocity[2, -1], 'py', split_axis=1, concat_axis=0, tiled=...]
  transfers between devices with their start and end apart: 30 -> 30, of which waited for: 3 -> 3; matrix products, arithmetic and copies ran while one was open for 21% -> 31% of each run, Pallas kernels for 0% -> 0%
where the time goes in v1:
time: 232 us; the launch traced here: 230 us
  starting transfers between devices  136 us (59%)
  local copies, waits for them, and re-layouts  48.3 us (21%)
  other arithmetic  37.5 us (16%)
  waiting for transfers between devices  6.45 us (3%)
    ppermute x6, starting transfers between devices, with_halo(): lax.ppermute(lax.slice_in_dim(block, 0, width, axis=dim), axis, backward)  38.9 us
    ppermute x6, starting transfers between devices, padded_2(): lax.ppermute(leading, axis, [(b, a) for a, b in up])  34.1 us
    unnamed x101, local copies, waits for them, and re-layouts  30 us
    all_to_all x3, starting transfers between devices, body(): lax.all_to_all(jnp.stack(jnp.split(row_data, lax.axis_size('py'), axis=1)...  20.2 us
    all_to_all x3, starting transfers between devices, body(): lax.all_to_all(air_field[0, 0], 'py', split_axis=1, concat_axis=0, tiled=...  17.7 us
    unnamed x18, other arithmetic  15.8 us
    ppermute x6, starting transfers between devices, with_halo(): lax.ppermute(lax.slice_in_dim(block, block.shape[dim] - width, None, axis...  13.1 us
    ppermute x6, starting transfers between devices, padded_2(): lax.ppermute(last, axis, up)  11.9 us
  transfers between devices with their start and end apart: 30, of which 3 were waited for; matrix products, arithmetic and copies ran while one was open for 31% of the time, Pallas kernels for 0%

profile of v1, /device:TPU:96, one launch (start us, length us, event | category | flops | bytes accessed | tf_op | source)
XLA Modules:
  0.0 230.1 jit_solution(958619615206197724)
XLA Ops:
  2.1 5.9 %all-to-all-start = ((f32[8,16,8]{2,0,1:T(8,128)}), f32[8,16,8]{2,0,1:T(8,128)S(1)}, u32[]{:S(2)}, u32[]{:S(2)}) async-start(f32[8,16,8]{2,0,1:T(8,128)} %copy.21), calls=%async_computation | async-start | bytes 131072 | tf_op jit(solution)/shard_map/all_to_all | solution.py:229
  11.3 5.6 %collective-permute-start.5 = (f32[6,16,1,128]{3,2,1,0:T(1,128)S(1)}, f32[6,16,1,128]{3,2,1,0:T(1,128)S(1)}, u32[]{:S(2)}, u32[]{:S(2)}) collective-permute-start(f32[6,16,1,128]{3,2,1,0:T(1,128)S(1)} %get-tuple-element.99), channel_id=1, source_target_pairs={{1,0},{2,1},{3,2},{4,3},{5,4},{6,5},{7,6},{8,7},{9,8},{10,9},{11,1... | collective-permute-start | bytes 147464 | tf_op jit(solution)/shard_map/ppermute | solution.py:31
  16.9 2.3 fusion.203
  19.2 3.4 %collective-permute-start = (f32[4,32,8,2]{3,2,1,0:T(8,128)}, f32[4,32,8,2]{3,2,1,0:T(8,128)S(1)}, u32[]{:S(2)}, u32[]{:S(2)}) collective-permute-start(f32[4,32,8,2]{3,2,1,0:T(8,128)} %get-tuple-element.92), channel_id=1, source_target_pairs={{0,16},{16,32},{32,48},{48,64},{64,80},{80,96},{96,112},{1,17},{17... | collective-permute-start | bytes 24584 | tf_op jit(solution)/shard_map/ppermute | solution.py:14
  22.6 6.1 %collective-permute-start.1 = (f32[4,32,8,2]{3,2,1,0:T(8,128)S(1)}, f32[4,32,8,2]{3,2,1,0:T(8,128)S(1)}, u32[]{:S(2)}, u32[]{:S(2)}) collective-permute-start(f32[4,32,8,2]{3,2,1,0:T(8,128)S(1)} %get-tuple-element.93), channel_id=1, source_target_pairs={{16,0},{32,16},{48,32},{64,48},{80,64},{96,80},{112,96},{17,1},{33... | collective-permute-start | bytes 24584 | tf_op jit(solution)/shard_map/ppermute | solution.py:17
  36.5 5.8 %collective-permute-start.11 = (f32[3,16,1,128]{3,2,1,0:T(1,128)S(1)}, f32[3,16,1,128]{3,2,1,0:T(1,128)S(1)}, u32[]{:S(2)}, u32[]{:S(2)}) collective-permute-start(f32[3,16,1,128]{3,2,1,0:T(1,128)S(1)} %get-tuple-element.119), channel_id=1, source_target_pairs={{1,0},{2,1},{3,2},{4,3},{5,4},{6,5},{7,6},{8,7},{9,8},{10,9},{11,1... | collective-permute-start | bytes 73736 | tf_op jit(solution)/shard_map/ppermute | solution.py:31
  52.8 7.6 %all-to-all-start.1 = ((f32[16,8,8]{2,1,0:T(8,128)}), f32[16,8,8]{2,1,0:T(8,128)S(1)}, u32[]{:S(2)}, u32[]{:S(2)}) async-start(f32[16,8,8]{2,1,0:T(8,128)} %constant_dynamic-update-slice_fusion), calls=%async_computation.1 | async-start | bytes 131072 | tf_op jit(solution)/shard_map/all_to_all | solution.py:236
  64.7 2.0 collective-permute-start.12
  66.8 5.6 %collective-permute-start.13 = (f32[6,16,1,128]{3,2,1,0:T(1,128)S(1)}, f32[6,16,1,128]{3,2,1,0:T(1,128)S(1)}, u32[]{:S(2)}, u32[]{:S(2)}) collective-permute-start(f32[6,16,1,128]{3,2,1,0:T(1,128)S(1)} %get-tuple-element.97), channel_id=1, source_target_pairs={{1,0},{2,1},{3,2},{4,3},{5,4},{6,5},{7,6},{8,7},{9,8},{10,9},{11,1... | collective-permute-start | bytes 147464 | tf_op jit(solution)/shard_map/ppermute | solution.py:31
  76.0 5.8 %collective-permute-start.3 = (f32[4,32,2,132]{3,2,1,0:T(2,128)}, f32[4,32,2,132]{3,2,1,0:T(2,128)}, u32[]{:S(2)}, u32[]{:S(2)}) collective-permute-start(f32[4,32,2,132]{3,2,1,0:T(2,128)} %get-tuple-element.67), channel_id=1, source_target_pairs={{1,0},{2,1},{3,2},{4,3},{5,4},{6,5},{7,6},{8,7},{9,8},{10,9},{11,1... | collective-permute-start | bytes 405512 | tf_op jit(solution)/shard_map/ppermute | solution.py:17
  86.0 2.0 pad_maximum_fusion
  91.0 5.9 %all-to-all-start.2 = ((f32[8,16,8]{2,0,1:T(8,128)}), f32[8,16,8]{2,0,1:T(8,128)S(1)}, u32[]{:S(2)}, u32[]{:S(2)}) async-start(f32[8,16,8]{2,0,1:T(8,128)} %copy.24), calls=%async_computation.2 | async-start | bytes 131072 | tf_op jit(solution)/shard_map/all_to_all | solution.py:229
  96.9 4.8 %all-to-all-done.2 = f32[8,16,8]{2,0,1:T(8,128)S(1)} async-done(((f32[8,16,8]{2,0,1:T(8,128)}), f32[8,16,8]{2,0,1:T(8,128)S(1)}, u32[]{:S(2)}, u32[]{:S(2)}) %all-to-all-start.2) | async-done | bytes 4128 | tf_op jit(solution)/shard_map/all_to_all | solution.py:229
  104.1 5.6 %collective-permute-start.19 = (f32[3,16,1,128]{3,2,1,0:T(1,128)S(1)}, f32[3,16,1,128]{3,2,1,0:T(1,128)S(1)}, u32[]{:S(2)}, u32[]{:S(2)}) collective-permute-start(f32[3,16,1,128]{3,2,1,0:T(1,128)S(1)} %get-tuple-element.117), channel_id=1, source_target_pairs={{1,0},{2,1},{3,2},{4,3},{5,4},{6,5},{7,6},{8,7},{9,8},{10,9},{11,1... | collective-permute-start | bytes 73736 | tf_op jit(solution)/shard_map/ppermute | solution.py:31
  120.3 6.8 %all-to-all-start.3 = ((f32[16,8,8]{2,1,0:T(8,128)}), f32[16,8,8]{2,1,0:T(8,128)S(1)}, u32[]{:S(2)}, u32[]{:S(2)}) async-start(f32[16,8,8]{2,1,0:T(8,128)} %constant_dynamic-update-slice_fusion.22), calls=%async_computation.3 | async-start | bytes 131072 | tf_op jit(solution)/shard_map/all_to_all | solution.py:236
  130.0 7.7 %collective-permute-start.7 = (f32[4,32,8,2]{3,2,1,0:T(8,128)S(1)}, f32[4,32,8,2]{3,2,1,0:T(8,128)S(1)}, u32[]{:S(2)}, u32[]{:S(2)}) collective-permute-start(f32[4,32,8,2]{3,2,1,0:T(8,128)S(1)} %get-tuple-element.88), channel_id=1, source_target_pairs={{16,0},{32,16},{48,32},{64,48},{80,64},{96,80},{112,96},{17,1},{33... | collective-permute-start | bytes 24584 | tf_op jit(solution)/shard_map/ppermute | solution.py:17
  146.8 5.8 %collective-permute-start.21 = (f32[6,16,1,128]{3,2,1,0:T(1,128)S(1)}, f32[6,16,1,128]{3,2,1,0:T(1,128)S(1)}, u32[]{:S(2)}, u32[]{:S(2)}) collective-permute-start(f32[6,16,1,128]{3,2,1,0:T(1,128)S(1)} %get-tuple-element.95), channel_id=1, source_target_pairs={{1,0},{2,1},{3,2},{4,3},{5,4},{6,5},{7,6},{8,7},{9,8},{10,9},{11,1... | collective-permute-start | bytes 147464 | tf_op jit(solution)/shard_map/ppermute | solution.py:31
  155.4 5.8 %collective-permute-start.9 = (f32[4,32,2,132]{3,2,1,0:T(2,128)S(1)}, f32[4,32,2,132]{3,2,1,0:T(2,128)S(1)}, u32[]{:S(2)}, u32[]{:S(2)}) collective-permute-start(f32[4,32,2,132]{3,2,1,0:T(2,128)S(1)} %get-tuple-element.65), channel_id=1, source_target_pairs={{1,0},{2,1},{3,2},{4,3},{5,4},{6,5},{7,6},{8,7},{9,8},{10,9},{11,1... | collective-permute-start | bytes 405512 | tf_op jit(solution)/shard_map/ppermute | solution.py:17
  169.1 5.9 %all-to-all-start.4 = ((f32[8,16,8]{2,0,1:T(8,128)}), f32[8,16,8]{2,0,1:T(8,128)S(1)}, u32[]{:S(2)}, u32[]{:S(2)}) async-start(f32[8,16,8]{2,0,1:T(8,128)} %copy.27), calls=%async_computation.4 | async-start | bytes 131072 | tf_op jit(solution)/shard_map/all_to_all | solution.py:229
  178.1 7.5 %collective-permute-start.15 = (f32[4,32,8,2]{3,2,1,0:T(8,128)}, f32[4,32,8,2]{3,2,1,0:T(8,128)S(1)}, u32[]{:S(2)}, u32[]{:S(2)}) collective-permute-start(f32[4,32,8,2]{3,2,1,0:T(8,128)} %get-tuple-element.83), channel_id=1, source_target_pairs={{16,0},{32,16},{48,32},{64,48},{80,64},{96,80},{112,96},{17,1},{33... | collective-permute-start | bytes 24584 | tf_op jit(solution)/shard_map/ppermute | solution.py:17
  197.9 5.7 %all-to-all-start.5 = ((f32[16,8,8]{2,1,0:T(8,128)}), f32[16,8,8]{2,1,0:T(8,128)S(1)}, u32[]{:S(2)}, u32[]{:S(2)}) async-start(f32[16,8,8]{2,1,0:T(8,128)} %constant_dynamic-update-slice_fusion.44), calls=%async_computation.5 | async-start | bytes 131072 | tf_op jit(solution)/shard_map/all_to_all | solution.py:236
  205.7 5.6 %collective-permute-start.23 = (f32[3,16,1,128]{3,2,1,0:T(1,128)S(1)}, f32[3,16,1,128]{3,2,1,0:T(1,128)S(1)}, u32[]{:S(2)}, u32[]{:S(2)}) collective-permute-start(f32[3,16,1,128]{3,2,1,0:T(1,128)S(1)} %get-tuple-element.115), channel_id=1, source_target_pairs={{1,0},{2,1},{3,2},{4,3},{5,4},{6,5},{7,6},{8,7},{9,8},{10,9},{11,1... | collective-permute-start | bytes 73736 | tf_op jit(solution)/shard_map/ppermute | solution.py:31
  212.3 2.1 collective-permute-start.16
  214.4 6.1 %collective-permute-start.17 = (f32[4,32,2,132]{3,2,1,0:T(2,128)S(1)}, f32[4,32,2,132]{3,2,1,0:T(2,128)S(1)}, u32[]{:S(2)}, u32[]{:S(2)}) collective-permute-start(f32[4,32,2,132]{3,2,1,0:T(2,128)S(1)} %get-tuple-element.57), channel_id=1, source_target_pairs={{1,0},{2,1},{3,2},{4,3},{5,4},{6,5},{7,6},{8,7},{9,8},{10,9},{11,1... | collective-permute-start | bytes 405512 | tf_op jit(solution)/shard_map/ppermute | solution.py:17
  (276 shorter events, 100.7 us)
Async XLA Ops:
  2.1 28.5 %all-to-all-start = ((f32[8,16,8]{2,0,1:T(8,128)}), f32[8,16,8]{2,0,1:T(8,128)S(1)}, u32[]{:S(2)}, u32[]{:S(2)}) async-start(f32[8,16,8]{2,0,1:T(8,128)} %copy.21), calls=%async_computation | async-start | bytes 131072 | tf_op jit(solution)/shard_map/all_to_all | solution.py:229
  9.2 21.4 %collective-permute-start.4 = (f32[6,16,1,128]{3,2,1,0:T(1,128)S(1)}, f32[6,16,1,128]{3,2,1,0:T(1,128)S(1)}, u32[]{:S(2)}, u32[]{:S(2)}) collective-permute-start(f32[6,16,1,128]{3,2,1,0:T(1,128)S(1)} %get-tuple-element.98), channel_id=1, source_target_pairs={{0,1},{1,2},{2,3},{3,4},{4,5},{5,6},{6,7},{7,8},{8,9},{9,10},{10,1... | collective-permute-start | bytes 147464 | tf_op jit(solution)/shard_map/ppermute | solution.py:30
  11.3 19.4 %collective-permute-start.5 = (f32[6,16,1,128]{3,2,1,0:T(1,128)S(1)}, f32[6,16,1,128]{3,2,1,0:T(1,128)S(1)}, u32[]{:S(2)}, u32[]{:S(2)}) collective-permute-start(f32[6,16,1,128]{3,2,1,0:T(1,128)S(1)} %get-tuple-element.99), channel_id=1, source_target_pairs={{1,0},{2,1},{3,2},{4,3},{5,4},{6,5},{7,6},{8,7},{9,8},{10,9},{11,1... | collective-permute-start | bytes 147464 | tf_op jit(solution)/shard_map/ppermute | solution.py:31
  19.2 53.2 %collective-permute-start = (f32[4,32,8,2]{3,2,1,0:T(8,128)}, f32[4,32,8,2]{3,2,1,0:T(8,128)S(1)}, u32[]{:S(2)}, u32[]{:S(2)}) collective-permute-start(f32[4,32,8,2]{3,2,1,0:T(8,128)} %get-tuple-element.92), channel_id=1, source_target_pairs={{0,16},{16,32},{32,48},{48,64},{64,80},{80,96},{96,112},{1,17},{17... | collective-permute-start | bytes 24584 | tf_op jit(solution)/shard_map/ppermute | solution.py:14
  22.6 49.8 %collective-permute-start.1 = (f32[4,32,8,2]{3,2,1,0:T(8,128)S(1)}, f32[4,32,8,2]{3,2,1,0:T(8,128)S(1)}, u32[]{:S(2)}, u32[]{:S(2)}) collective-permute-start(f32[4,32,8,2]{3,2,1,0:T(8,128)S(1)} %get-tuple-element.93), channel_id=1, source_target_pairs={{16,0},{32,16},{48,32},{64,48},{80,64},{96,80},{112,96},{17,1},{33... | collective-permute-start | bytes 24584 | tf_op jit(solution)/shard_map/ppermute | solution.py:17
  34.6 25.8 %collective-permute-start.10 = (f32[3,16,1,128]{3,2,1,0:T(1,128)S(1)}, f32[3,16,1,128]{3,2,1,0:T(1,128)S(1)}, u32[]{:S(2)}, u32[]{:S(2)}) collective-permute-start(f32[3,16,1,128]{3,2,1,0:T(1,128)S(1)} %get-tuple-element.118), channel_id=1, source_target_pairs={{0,1},{1,2},{2,3},{3,4},{4,5},{5,6},{6,7},{7,8},{8,9},{9,10},{10,1... | collective-permute-start | bytes 73736 | tf_op jit(solution)/shard_map/ppermute | solution.py:30
  36.5 23.9 %collective-permute-start.11 = (f32[3,16,1,128]{3,2,1,0:T(1,128)S(1)}, f32[3,16,1,128]{3,2,1,0:T(1,128)S(1)}, u32[]{:S(2)}, u32[]{:S(2)}) collective-permute-start(f32[3,16,1,128]{3,2,1,0:T(1,128)S(1)} %get-tuple-element.119), channel_id=1, source_target_pairs={{1,0},{2,1},{3,2},{4,3},{5,4},{6,5},{7,6},{8,7},{9,8},{10,9},{11,1... | collective-permute-start | bytes 73736 | tf_op jit(solution)/shard_map/ppermute | solution.py:31
  52.8 29.0 %all-to-all-start.1 = ((f32[16,8,8]{2,1,0:T(8,128)}), f32[16,8,8]{2,1,0:T(8,128)S(1)}, u32[]{:S(2)}, u32[]{:S(2)}) async-start(f32[16,8,8]{2,1,0:T(8,128)} %constant_dynamic-update-slice_fusion), calls=%async_computation.1 | async-start | bytes 131072 | tf_op jit(solution)/shard_map/all_to_all | solution.py:236
  64.7 17.7 %collective-permute-start.12 = (f32[6,16,1,128]{3,2,1,0:T(1,128)S(1)}, f32[6,16,1,128]{3,2,1,0:T(1,128)S(1)}, u32[]{:S(2)}, u32[]{:S(2)}) collective-permute-start(f32[6,16,1,128]{3,2,1,0:T(1,128)S(1)} %get-tuple-element.96), channel_id=1, source_target_pairs={{0,1},{1,2},{2,3},{3,4},{4,5},{5,6},{6,7},{7,8},{8,9},{9,10},{10,1... | collective-permute-start | bytes 147464 | tf_op jit(solution)/shard_map/ppermute | solution.py:30
  66.8 15.7 %collective-permute-start.13 = (f32[6,16,1,128]{3,2,1,0:T(1,128)S(1)}, f32[6,16,1,128]{3,2,1,0:T(1,128)S(1)}, u32[]{:S(2)}, u32[]{:S(2)}) collective-permute-start(f32[6,16,1,128]{3,2,1,0:T(1,128)S(1)} %get-tuple-element.97), channel_id=1, source_target_pairs={{1,0},{2,1},{3,2},{4,3},{5,4},{6,5},{7,6},{8,7},{9,8},{10,9},{11,1... | collective-permute-start | bytes 147464 | tf_op jit(solution)/shard_map/ppermute | solution.py:31
  102.0 36.4 %collective-permute-start.18 = (f32[3,16,1,128]{3,2,1,0:T(1,128)S(1)}, f32[3,16,1,128]{3,2,1,0:T(1,128)S(1)}, u32[]{:S(2)}, u32[]{:S(2)}) collective-permute-start(f32[3,16,1,128]{3,2,1,0:T(1,128)S(1)} %get-tuple-element.116), channel_id=1, source_target_pairs={{0,1},{1,2},{2,3},{3,4},{4,5},{5,6},{6,7},{7,8},{8,9},{9,10},{10,1... | collective-permute-start | bytes 73736 | tf_op jit(solution)/shard_map/ppermute | solution.py:30
  104.1 34.3 %collective-permute-start.19 = (f32[3,16,1,128]{3,2,1,0:T(1,128)S(1)}, f32[3,16,1,128]{3,2,1,0:T(1,128)S(1)}, u32[]{:S(2)}, u32[]{:S(2)}) collective-permute-start(f32[3,16,1,128]{3,2,1,0:T(1,128)S(1)} %get-tuple-element.117), channel_id=1, source_target_pairs={{1,0},{2,1},{3,2},{4,3},{5,4},{6,5},{7,6},{8,7},{9,8},{10,9},{11,1... | collective-permute-start | bytes 73736 | tf_op jit(solution)/shard_map/ppermute | solution.py:31
  120.3 17.5 %all-to-all-start.3 = ((f32[16,8,8]{2,1,0:T(8,128)}), f32[16,8,8]{2,1,0:T(8,128)S(1)}, u32[]{:S(2)}, u32[]{:S(2)}) async-start(f32[16,8,8]{2,1,0:T(8,128)} %constant_dynamic-update-slice_fusion.22), calls=%async_computation.3 | async-start | bytes 131072 | tf_op jit(solution)/shard_map/all_to_all | solution.py:236
  128.1 24.5 %collective-permute-start.6 = (f32[4,32,8,2]{3,2,1,0:T(8,128)}, f32[4,32,8,2]{3,2,1,0:T(8,128)S(1)}, u32[]{:S(2)}, u32[]{:S(2)}) collective-permute-start(f32[4,32,8,2]{3,2,1,0:T(8,128)} %get-tuple-element.87), channel_id=1, source_target_pairs={{0,16},{16,32},{32,48},{48,64},{64,80},{80,96},{96,112},{1,17},{17... | collective-permute-start | bytes 24584 | tf_op jit(solution)/shard_map/ppermute | solution.py:14
  130.0 22.6 %collective-permute-start.7 = (f32[4,32,8,2]{3,2,1,0:T(8,128)S(1)}, f32[4,32,8,2]{3,2,1,0:T(8,128)S(1)}, u32[]{:S(2)}, u32[]{:S(2)}) collective-permute-start(f32[4,32,8,2]{3,2,1,0:T(8,128)S(1)} %get-tuple-element.88), channel_id=1, source_target_pairs={{16,0},{32,16},{48,32},{64,48},{80,64},{96,80},{112,96},{17,1},{33... | collective-permute-start | bytes 24584 | tf_op jit(solution)/shard_map/ppermute | solution.py:17
  144.9 16.3 %collective-permute-start.20 = (f32[6,16,1,128]{3,2,1,0:T(1,128)S(1)}, f32[6,16,1,128]{3,2,1,0:T(1,128)S(1)}, u32[]{:S(2)}, u32[]{:S(2)}) collective-permute-start(f32[6,16,1,128]{3,2,1,0:T(1,128)S(1)} %get-tuple-element.94), channel_id=1, source_target_pairs={{0,1},{1,2},{2,3},{3,4},{4,5},{5,6},{6,7},{7,8},{8,9},{9,10},{10,1... | collective-permute-start | bytes 147464 | tf_op jit(solution)/shard_map/ppermute | solution.py:30
  146.8 14.4 %collective-permute-start.21 = (f32[6,16,1,128]{3,2,1,0:T(1,128)S(1)}, f32[6,16,1,128]{3,2,1,0:T(1,128)S(1)}, u32[]{:S(2)}, u32[]{:S(2)}) collective-permute-start(f32[6,16,1,128]{3,2,1,0:T(1,128)S(1)} %get-tuple-element.95), channel_id=1, source_target_pairs={{1,0},{2,1},{3,2},{4,3},{5,4},{6,5},{7,6},{8,7},{9,8},{10,9},{11,1... | collective-permute-start | bytes 147464 | tf_op jit(solution)/shard_map/ppermute | solution.py:31
  169.1 16.5 %all-to-all-start.4 = ((f32[8,16,8]{2,0,1:T(8,128)}), f32[8,16,8]{2,0,1:T(8,128)S(1)}, u32[]{:S(2)}, u32[]{:S(2)}) async-start(f32[8,16,8]{2,0,1:T(8,128)} %copy.27), calls=%async_computation.4 | async-start | bytes 131072 | tf_op jit(solution)/shard_map/all_to_all | solution.py:229
  176.2 35.3 %collective-permute-start.14 = (f32[4,32,8,2]{3,2,1,0:T(8,128)}, f32[4,32,8,2]{3,2,1,0:T(8,128)S(1)}, u32[]{:S(2)}, u32[]{:S(2)}) collective-permute-start(f32[4,32,8,2]{3,2,1,0:T(8,128)} %get-tuple-element.82), channel_id=1, source_target_pairs={{0,16},{16,32},{32,48},{48,64},{64,80},{80,96},{96,112},{1,17},{17... | collective-permute-start | bytes 24584 | tf_op jit(solution)/shard_map/ppermute | solution.py:14
  178.1 33.3 %collective-permute-start.15 = (f32[4,32,8,2]{3,2,1,0:T(8,128)}, f32[4,32,8,2]{3,2,1,0:T(8,128)S(1)}, u32[]{:S(2)}, u32[]{:S(2)}) collective-permute-start(f32[4,32,8,2]{3,2,1,0:T(8,128)} %get-tuple-element.83), channel_id=1, source_target_pairs={{16,0},{32,16},{48,32},{64,48},{80,64},{96,80},{112,96},{17,1},{33... | collective-permute-start | bytes 24584 | tf_op jit(solution)/shard_map/ppermute | solution.py:17
  197.9 13.4 %all-to-all-start.5 = ((f32[16,8,8]{2,1,0:T(8,128)}), f32[16,8,8]{2,1,0:T(8,128)S(1)}, u32[]{:S(2)}, u32[]{:S(2)}) async-start(f32[16,8,8]{2,1,0:T(8,128)} %constant_dynamic-update-slice_fusion.44), calls=%async_computation.5 | async-start | bytes 131072 | tf_op jit(solution)/shard_map/all_to_all | solution.py:236
  203.7 16.9 %collective-permute-start.22 = (f32[3,16,1,128]{3,2,1,0:T(1,128)S(1)}, f32[3,16,1,128]{3,2,1,0:T(1,128)S(1)}, u32[]{:S(2)}, u32[]{:S(2)}) collective-permute-start(f32[3,16,1,128]{3,2,1,0:T(1,128)S(1)} %get-tuple-element.114), channel_id=1, source_target_pairs={{0,1},{1,2},{2,3},{3,4},{4,5},{5,6},{6,7},{7,8},{8,9},{9,10},{10,1... | collective-permute-start | bytes 73736 | tf_op jit(solution)/shard_map/ppermute | solution.py:30
  205.7 14.8 %collective-permute-start.23 = (f32[3,16,1,128]{3,2,1,0:T(1,128)S(1)}, f32[3,16,1,128]{3,2,1,0:T(1,128)S(1)}, u32[]{:S(2)}, u32[]{:S(2)}) collective-permute-start(f32[3,16,1,128]{3,2,1,0:T(1,128)S(1)} %get-tuple-element.115), channel_id=1, source_target_pairs={{1,0},{2,1},{3,2},{4,3},{5,4},{6,5},{7,6},{8,7},{9,8},{10,9},{11,1... | collective-permute-start | bytes 73736 | tf_op jit(solution)/shard_map/ppermute | solution.py:31
  212.3 13.7 %collective-permute-start.16 = (f32[4,32,2,132]{3,2,1,0:T(2,128)S(1)}, f32[4,32,2,132]{3,2,1,0:T(2,128)S(1)}, u32[]{:S(2)}, u32[]{:S(2)}) collective-permute-start(f32[4,32,2,132]{3,2,1,0:T(2,128)S(1)} %get-tuple-element.56), channel_id=1, source_target_pairs={{0,1},{1,2},{2,3},{3,4},{4,5},{5,6},{6,7},{7,8},{8,9},{9,10},{10,1... | collective-permute-start | bytes 405512 | tf_op jit(solution)/shard_map/ppermute | solution.py:14
  (34 other events, 250.3 us)
